TPU v7x, 32 devices: a whole 2x2x4 slice. The times are simulated.
32 devices in a mesh: dp: 4 (over y, core), expert: 8 (over z, x).
Axes of the slice: x: 2, y: 2, z: 4, core: 2. Of those that a mesh axis runs over, the one named last changes fastest.
Arguments:
- tokens: bfloat16 [4096, 2048], P(('dp', 'expert')), may hold values from -6 to 6
- expert_ids: int32 [4096, 4], P(('dp', 'expert')), may hold values from 0 to 31, as said below
- gate_weights: float32 [4096, 4], P(('dp', 'expert')), may hold values from 0.02 to 0.5
- w_gate: bfloat16 [32, 2048, 768], P('expert', 'dp'), may hold values from -0.125 to 0.125
- w_up: bfloat16 [32, 2048, 768], P('expert', 'dp'), may hold values from -0.125 to 0.125
- w_down: bfloat16 [32, 768, 2048], P('expert', None, 'dp'), may hold values from -0.21875 to 0.21875
Outputs:
- combined: bfloat16 [4096, 2048], P(('dp', 'expert'))
Inputs may be any that keep to these rules, and one draw needn't show every extreme that they name: `expert_ids`: each row names 4 different experts. The rows of one device name no expert more than 24 times; in every dp group two experts are named exactly 24 times by the rows of each of its devices.
All inputs are finite; a program needn't handle non-finite values.
Results may differ from a plain program's by a relative error of at most 0.0057.
Values may be sent and summed in bfloat16 or wider, within the bound.
No kernel may reach another device: no remote copies, remote signals or barrier semaphores. Data moves between devices by JAX's collectives and lax.ppermute only.
A program may use at most 128 MiB of HBM per device.

v0:
```python
import jax
import jax.numpy as jnp
from jax import lax
from jax.sharding import PartitionSpec as P


def expert_layer(expert_rows, gate_full, up_full, down_full):
    gate_sum = jnp.einsum(
        "erd,edf->erf", expert_rows, gate_full, preferred_element_type=jnp.float32
    )
    up_sum = jnp.einsum("erd,edf->erf", expert_rows, up_full, preferred_element_type=jnp.float32)
    hidden = (jax.nn.silu(gate_sum) * up_sum).astype(jnp.bfloat16)
    return jnp.einsum("erf,efd->erd", hidden, down_full, preferred_element_type=jnp.float32).astype(
        jnp.bfloat16
    )


def on_device(tokens, expert_ids, gate_weights, w_gate, w_up, w_down):
    members = lax.axis_size("expert")
    tok_count = tokens.shape[0]
    model_width = tokens.shape[1]
    top_count = expert_ids.shape[1]
    local_experts = w_gate.shape[0]
    capacity = tok_count * 3 // 16
    total_experts = members * local_experts
    buffer_rows = total_experts * capacity
    flat_ids = expert_ids.reshape(-1)
    one_hot = (flat_ids[:, None] == jnp.arange(total_experts, dtype=jnp.int32)[None, :]).astype(
        jnp.int32
    )
    earlier = jnp.cumsum(one_hot, axis=0) - one_hot
    slot_index = jnp.sum(earlier * one_hot, axis=1)
    owner_dev = flat_ids // local_experts
    local_index = flat_ids % local_experts
    target = (local_index * members + owner_dev) * capacity + slot_index
    token_of = jnp.arange(flat_ids.shape[0], dtype=jnp.int32) // top_count
    source_row = jnp.zeros((buffer_rows,), jnp.int32).at[target].set(token_of)
    filled = jnp.zeros((buffer_rows,), jnp.bool_).at[target].set(True)
    outgoing = jnp.where(filled[:, None], tokens[source_row], jnp.zeros((), tokens.dtype))
    outgoing = outgoing.reshape(local_experts, members, capacity, model_width)
    incoming = lax.all_to_all(outgoing, "expert", split_axis=1, concat_axis=1, tiled=True)
    expert_rows = incoming.reshape(local_experts, members * capacity, model_width)
    gate_full, up_full = (
        lax.all_gather(w_gate, "dp", axis=1, tiled=True),
        lax.all_gather(w_up, "dp", axis=1, tiled=True),
    )
    down_full = lax.all_gather(w_down, "dp", axis=2, tiled=True)
    results = expert_layer(expert_rows, gate_full, up_full, down_full)
    returned = lax.all_to_all(
        results.reshape(local_experts, members, capacity, model_width),
        "expert",
        split_axis=1,
        concat_axis=1,
        tiled=True,
    )
    flat_back = returned.reshape(buffer_rows, model_width)
    picked = flat_back[target].reshape(tok_count, top_count, model_width).astype(jnp.float32)
    combined = jnp.sum(gate_weights[:, :, None] * picked, axis=1)
    return combined.astype(jnp.bfloat16)


def solution(mesh):
    in_specs = (
        P(("dp", "expert"), None),
        P(("dp", "expert"), None),
        P(("dp", "expert"), None),
        P("expert", "dp", None),
        P("expert", "dp", None),
        P("expert", None, "dp"),
    )
    out_specs = P(("dp", "expert"), None)
    return jax.shard_map(
        on_device, mesh=mesh, in_specs=in_specs, out_specs=out_specs, check_vma=False
    )
```

profile of v0, /device:TPU:0, one launch (start us, length us, event | category | flops | bytes accessed | tf_op | source)
XLA Modules:
  0.0 380.7 jit_solution(11069412516284014962)
XLA Ops:
  6.5 0.7 all-gather.4.cloned.1.call-update
  7.3 0.0 all-gather.6.cloned.1.call-start
  7.3 0.7 all-gather.6.cloned.1.call-update
  8.0 0.0 all-gather.8.cloned.1.call-start
  8.1 0.7 all-gather.8.cloned.1.call-update
  8.8 0.1 copy.23
  8.9 0.1 eq.31
  9.0 0.1 eq.27
  9.1 0.1 reshape.161
  9.2 1.2 reduce-window.6
  10.4 0.2 slice_reduce_fusion
  10.7 0.1 fusion.3
  10.8 2.4 scatter_custom_fusion.1
  13.3 2.4 scatter_custom_fusion
  15.7 0.1 broadcast_in_dim.31
  15.9 4.3 %gather_fusion = bf16[768,2048]{1,0:T(8,128)(2,1)} fusion(bf16[128,2048]{1,0:T(8,128)(2,1)S(1)} %copy-done, s32[1024]{0:T(1024)S(1)} %pad_clamp_fusion.1), kind=kCustom, calls=%fused_computation | custom fusion | bytes 6294528 | tf_op jit(solution)/shard_map/gather | solution.py:39
  20.1 2.7 copy_select_fusion
  22.9 77.7 %all_to_all.10 = bf16[4,8,24,2048]{3,2,0,1:T(8,128)(2,1)S(1)} all-to-all(bf16[4,8,24,2048]{3,2,0,1:T(8,128)(2,1)S(1)} %copy_select_fusion), channel_id=1, replica_groups=mesh['dp'=4,'expert'=8] {'expert'}, dimensions={1} | all-to-all | bytes 6291456 | tf_op jit(solution)/shard_map/all_to_all | solution.py:41
  100.6 0.2 copy.29
  100.8 0.0 all-gather.4.cloned.1.call-done
  100.9 10.5 %fusion.15 = f32[4,192,768]{2,1,0:T(8,128)} fusion(bf16[4,192,2048]{2,1,0:T(8,128)(2,1)S(1)} %bitcast.31, bf16[4,2048,768]{2,1,0:T(8,128)(2,1)} %all-gather.4.cloned.1.call-done), kind=kOutput, calls=%fused_computation.41 | convolution fusion | flops 2415919104 | bytes 18087936 | tf_op jit(solution)/shard_map/erd,edf->erf/dot_general | solution.py:8
  111.4 66.0 %all-gather.6.cloned.1.call-done = bf16[4,2048,768]{2,1,0:T(8,128)(2,1)} async-done(((bf16[4,512,768]{2,1,0:T(8,128)(2,1)}), bf16[4,2048,768]{2,1,0:T(8,128)(2,1)}) %all-gather.6.cloned.1.call-update) | async-done | bytes 12582928 | tf_op jit(solution)/shard_map/all_gather | solution.py:45
  177.4 83.7 %all-gather.8.cloned.1.call-done = bf16[4,768,2048]{2,1,0:T(8,128)(2,1)} async-done(((bf16[4,768,512]{2,1,0:T(8,128)(2,1)}), bf16[4,768,2048]{2,1,0:T(8,128)(2,1)}) %all-gather.8.cloned.1.call-update) | async-done | bytes 12582928 | tf_op jit(solution)/shard_map/all_gather | solution.py:47
  261.1 15.8 %convolution_convert_fusion = bf16[4,192,2048]{2,1,0:T(8,128)(2,1)} fusion(bf16[4,768,2048]{2,1,0:T(8,128)(2,1)} %all-gather.8.cloned.1.call-done, f32[4,192,768]{2,1,0:T(8,128)} %fusion.15, bf16[4,192,2048]{2,1,0:T(8,128)(2,1)S(1)} %bitcast.32, bf16[4,2048,768]{2,1,0:T(8,128)(2,1)} %all-gather.6.cloned.1.call-done), kind=kOutput, calls=%fused_computation.5 | convolution fusion | flops 4836950016 | bytes 33816576 | tf_op jit(solution)/shard_map/erf,efd->erd/dot_general | solution.py:13
  276.9 4.0 %copy.30 = bf16[4,8,24,2048]{3,2,0,1:T(8,128)(2,1)} copy(bf16[4,8,24,2048]{3,2,1,0:T(8,128)(2,1)} %bitcast.34) | data formatting | bytes 6291456 | tf_op jit(solution)/shard_map/reshape | solution.py:50
  280.9 5.6 %all-to-all-start.1 = ((bf16[4,8,24,2048]{3,2,0,1:T(8,128)(2,1)}), bf16[4,8,24,2048]{3,2,0,1:T(8,128)(2,1)}, u32[]{:S(2)}, u32[]{:S(2)}) async-start(bf16[4,8,24,2048]{3,2,0,1:T(8,128)(2,1)} %copy.30), calls=%async_computation.1 | async-start | bytes 6291456 | tf_op jit(solution)/shard_map/all_to_all | solution.py:49
  286.5 0.1 copy.22
  286.6 71.1 %all-to-all-done.1 = bf16[4,8,24,2048]{3,2,0,1:T(8,128)(2,1)} async-done(((bf16[4,8,24,2048]{3,2,0,1:T(8,128)(2,1)}), bf16[4,8,24,2048]{3,2,0,1:T(8,128)(2,1)}, u32[]{:S(2)}, u32[]{:S(2)}) %all-to-all-start.1) | async-done | bytes 3145760 | tf_op jit(solution)/shard_map/all_to_all | solution.py:49
  357.7 2.1 copy.31
  359.8 3.3 gather_fusion.1
  363.2 4.8 %reshape.166 = f32[128,4,2048]{2,1,0:T(4,128)} reshape(bf16[512,2048]{1,0:T(8,128)(2,1)} %gather_fusion.1) | data formatting | bytes 6291456 | tf_op jit(solution)/shard_map/convert_element_type | solution.py:57
  368.0 6.2 %multiply_reduce_fusion = bf16[128,2048]{1,0:T(8,128)(2,1)} fusion(f32[128,4,2048]{2,1,0:T(4,128)} %reshape.166, f32[128,4]{1,0:T(8,128)S(1)} %copy.22), kind=kLoop, calls=%fused_computation.4 | loop fusion | flops 1835008 | bytes 4720640 | tf_op jit(solution)/shard_map/reduce_sum | solution.py:58
  (19 shorter events, 0.1 us)
Async XLA Ops:
  6.5 9.3 %copy-start = (bf16[128,2048]{1,0:T(8,128)(2,1)S(1)}, bf16[128,2048]{1,0:T(8,128)(2,1)}, u32[]{:S(2)}) copy-start(bf16[128,2048]{1,0:T(8,128)(2,1)} %param.6) | copy-start | bytes 1572868
  6.5 94.3 %all-gather.4.cloned.1.call-start = ((), (), s32[]{:S(2)}) async-start(), calls=%async_computation.2 | async-start | bytes 15728640 | tf_op jit(solution)/shard_map/all_gather | solution.py:44
  7.3 1.5 copy-start.2
  7.3 170.2 %all-gather.6.cloned.1.call-start = ((), (), s32[]{:S(2)}) async-start(), calls=%async_computation.3 | async-start | bytes 15728640 | tf_op jit(solution)/shard_map/all_gather | solution.py:45
  8.0 253.1 %all-gather.8.cloned.1.call-start = ((), (), s32[]{:S(2)}) async-start(), calls=%async_computation.4 | async-start | bytes 15728640 | tf_op jit(solution)/shard_map/all_gather | solution.py:47
  280.8 5.6 %copy-start.3 = (f32[128,4]{0,1:T(4,128)S(1)}, f32[128,4]{0,1:T(4,128)}, u32[]{:S(2)}) copy-start(f32[128,4]{0,1:T(4,128)} %param.8) | copy-start | bytes 6148
  280.9 76.9 %all-to-all-start.1 = ((bf16[4,8,24,2048]{3,2,0,1:T(8,128)(2,1)}), bf16[4,8,24,2048]{3,2,0,1:T(8,128)(2,1)}, u32[]{:S(2)}, u32[]{:S(2)}) async-start(bf16[4,8,24,2048]{3,2,0,1:T(8,128)(2,1)} %copy.30), calls=%async_computation.1 | async-start | bytes 6291456 | tf_op jit(solution)/shard_map/all_to_all | solution.py:49
  363.2 11.0 %copy-start.1 = (bf16[128,2048]{1,0:T(8,128)(2,1)S(1)}, bf16[128,2048]{1,0:T(8,128)(2,1)}, u32[]{:S(2)}) copy-start(bf16[128,2048]{1,0:T(8,128)(2,1)} %param.6) | copy-start | bytes 1572868
Sparse Core Ops, SparseCore 0:
  8.9 84.8 all-gather.3
  95.3 82.0 all-gather.5
  179.0 82.0 all-gather.7
where the time goes:
time: 381 us
  waiting for transfers between devices  223 us (59%)
  blocking collectives  77.7 us (20%)
  matrix products  26.3 us (7%)
  local copies, waits for them, and re-layouts  24.5 us (6%)
  between operations  13.2 us (3%)
  other arithmetic  10.3 us (3%)
  starting transfers between devices  5.72 us (2%)
    all_gather x1, waiting for transfers between devices, on_device(): down_full = lax.all_gather(w_down, 'dp', axis=2, tiled=True)  83.7 us
    all_to_all x1, blocking collectives, on_device(): lax.all_to_all(outgoing, 'expert', split_axis=1, concat_axis=1, tiled=True)  77.7 us
    all_to_all x1, waiting for transfers between devices, on_device(): lax.all_to_all(results.reshape(local_experts, members, capacity, model_wi...  71.1 us
    all_gather x1, waiting for transfers between devices, on_device(): lax.all_gather(w_up, 'dp', axis=1, tiled=True)  66 us
    dot_general x1, matrix products, expert_layer(): jnp.einsum('erf,efd->erd', hidden, down_full, preferred_element_type=jnp....  15.8 us
    dot_general x1, matrix products, expert_layer(): jnp.einsum('erd,edf->erf', expert_rows, gate_full, preferred_element_type...  10.5 us
  transfers between devices with their start and end apart: 4, of which 3 were waited for; matrix products, arithmetic and copies ran while one was open for 7% of the time, Pallas kernels for 0%

commit v1 on v0

--- a/solution.py
+++ b/solution.py
@@ -1,7 +1,14 @@
+import functools
+
 import jax
 import jax.numpy as jnp
 from jax import lax
+from jax.experimental import pallas as pl
+from jax.experimental.pallas import tpu as pltpu
 from jax.sharding import PartitionSpec as P
+
+BF16 = jnp.bfloat16
+F32 = jnp.float32
 
 
 def expert_layer(expert_rows, gate_full, up_full, down_full):
@@ -15,7 +22,7 @@
     )
 
 
-def on_device(tokens, expert_ids, gate_weights, w_gate, w_up, w_down):
+def gathered_weights(tokens, expert_ids, gate_weights, w_gate, w_up, w_down):
     members = lax.axis_size("expert")
     tok_count = tokens.shape[0]
     model_width = tokens.shape[1]
@@ -59,6 +66,233 @@
     return combined.astype(jnp.bfloat16)
 
 
+def slots_of(info_refs, base, top, experts, cap):
+    hits = []
+    for g in range(2):
+        for ref in info_refs:
+            ids = ref[g, :top, :]
+            for e in range(experts):
+                want = (base + e).astype(F32)
+                hits.append(jnp.max(jnp.where(ids == want, 1.0, 0.0), axis=0, keepdims=True))
+    hit = jnp.concatenate(hits, axis=0)
+    tok = hit.shape[1]
+    before = lax.broadcasted_iota(jnp.int32, (tok, tok), 0) < lax.broadcasted_iota(
+        jnp.int32, (tok, tok), 1
+    )
+    order = jnp.dot(
+        hit.astype(BF16), jnp.where(before, 1.0, 0.0).astype(BF16), preferred_element_type=F32
+    )
+    slots = {}
+    at = 0
+    for g in range(2):
+        for s in range(len(info_refs)):
+            for e in range(experts):
+                row = jnp.where(hit[at : at + 1] > 0.5, order[at : at + 1] + float(s * cap), -1.0)
+                slots[g, s, e] = row.astype(jnp.int32)
+                at += 1
+    return slots
+
+
+def rows_kernel(
+    cap, top, place, info_a, info_b, tok_a, tok_b, wg_own, wg_oth, wu_own, wu_oth,
+    send, keep, rows,
+):
+    core, base = place[0], place[1]
+    e = pl.program_id(0)
+    experts = rows.shape[0]
+    both = 2 * cap
+    quarter = wg_own.shape[1]
+    width = wg_own.shape[2]
+
+    @pl.when(e == 0)
+    def _():
+        slots = slots_of((info_a, info_b), base, top, experts, cap)
+        tok = tok_a.shape[1]
+        row_id = lax.broadcasted_iota(jnp.int32, (both, tok), 0)
+        for g in range(2):
+            total = None
+            for s, tref in enumerate((tok_a, tok_b)):
+                pick = jnp.concatenate(
+                    [jnp.where(row_id == slots[g, s, q], 1.0, 0.0) for q in range(experts)], axis=0
+                ).astype(BF16)
+                part = jnp.dot(pick, tref[g], preferred_element_type=F32)
+                total = part if total is None else total + part
+            total = total.astype(BF16)
+            for q in range(experts):
+                rows[q, g * both : (g + 1) * both, :] = total[q * both : (q + 1) * both]
+
+    own = rows[e, :, pl.ds(pl.multiple_of(core * quarter, quarter), quarter)]
+    oth = rows[e, :, pl.ds(pl.multiple_of((1 - core) * quarter, quarter), quarter)]
+    for at, (wo, wt) in enumerate(((wg_own, wg_oth), (wu_own, wu_oth))):
+        total = jnp.dot(own, wo[0], preferred_element_type=F32) + jnp.dot(
+            oth, wt[0], preferred_element_type=F32
+        )
+        keep[0, :, at * width : (at + 1) * width] = total[:both]
+        send[0, :, at * width : (at + 1) * width] = total[both:].astype(BF16)
+
+
+def down_kernel(
+    cap, top, place, info_a, info_b, hid_own, hid_par, wd_own, wd_oth, send, keep, outs
+):
+    core, base = place[0], place[1]
+    e = pl.program_id(0)
+    experts = pl.num_programs(0)
+    both = 2 * cap
+    quarter = wd_own.shape[2]
+    hid = jnp.concatenate([hid_own[0], hid_par[0]], axis=0)
+    for col, w in ((core, wd_own), (1 - core, wd_oth)):
+        out = jnp.dot(hid, w[0], preferred_element_type=F32).astype(BF16)
+        cols = pl.ds(pl.multiple_of(col * quarter, quarter), quarter)
+        at = pl.ds(pl.multiple_of(e * both, both), both)
+        outs[0, at, cols] = out[:both]
+        outs[1, at, cols] = out[both:]
+
+    @pl.when(e == experts - 1)
+    def _():
+        count = outs.shape[1] // both
+        slots = slots_of((info_a, info_b), base, top, count, cap)
+        tok = info_a.shape[2]
+        row_id = lax.broadcasted_iota(jnp.int32, (both, tok), 0)
+        for g in range(2):
+            for s, (ref, dest) in enumerate(((info_a, keep), (info_b, send))):
+                ids = ref[g, :top, :]
+                scale = ref[g, top : 2 * top, :]
+                parts = []
+                for q in range(count):
+                    want = (base + q).astype(F32)
+                    weight = jnp.sum(jnp.where(ids == want, scale, 0.0), axis=0, keepdims=True)
+                    parts.append(jnp.where(row_id == slots[g, s, q], weight, 0.0))
+                spread = jnp.concatenate(parts, axis=0)
+                high = spread.astype(BF16)
+                low = (spread - high.astype(F32)).astype(BF16)
+                dims = (((0,), (0,)), ((), ()))
+                total = lax.dot_general(high, outs[g], dims, preferred_element_type=F32)
+                total = total + lax.dot_general(low, outs[g], dims, preferred_element_type=F32)
+                dest[g] = total.astype(dest.dtype)
+
+
+def whole(shape):
+    return pl.BlockSpec(shape, lambda e, place: (0,) * len(shape))
+
+
+def slab(shape):
+    return pl.BlockSpec((1,) + tuple(shape[1:]), lambda e, place: (e,) + (0,) * (len(shape) - 1))
+
+
+def call(kernel, name, grid, place, fulls, slabs, outs_full, outs_slab, scratch, flops):
+    operands = fulls + slabs
+    out_shape = outs_full + outs_slab
+    moved = sum(a.size * a.dtype.itemsize for a in operands) + sum(
+        a.size * jnp.dtype(a.dtype).itemsize for a in out_shape
+    )
+    return pl.pallas_call(
+        kernel,
+        name=name,
+        out_shape=out_shape,
+        grid_spec=pltpu.PrefetchScalarGridSpec(
+            num_scalar_prefetch=1,
+            grid=(grid,),
+            in_specs=[whole(a.shape) for a in fulls] + [slab(a.shape) for a in slabs],
+            out_specs=[whole(a.shape) for a in outs_full] + [slab(a.shape) for a in outs_slab],
+            scratch_shapes=scratch,
+        ),
+        compiler_params=pltpu.CompilerParams(dimension_semantics=("arbitrary",)),
+        cost_estimate=pl.CostEstimate(flops=flops, bytes_accessed=moved, transcendentals=0),
+    )(place, *operands)
+
+
+def local_weights(tokens, expert_ids, gate_weights, w_gate, w_up, w_down):
+    members = lax.axis_size("expert")
+    planes = members // 2
+    tok, width = tokens.shape
+    top = expert_ids.shape[1]
+    experts, quarter, hidden_width = w_gate.shape
+    half = 2 * quarter
+    cap = tok * 3 // 16
+    both = 2 * cap
+    i = lax.axis_index("dp")
+    j = lax.axis_index("expert")
+    side, core = i // 2, i % 2
+    place = jnp.stack([core, j * experts]).astype(jnp.int32)
+
+    def across(x):
+        return lax.ppermute(x, "dp", [(d, d ^ 2) for d in range(4)])
+
+    def cores(x):
+        return lax.ppermute(x, "dp", [(d, d ^ 1) for d in range(4)])
+
+    def flip(x):
+        return lax.ppermute(x, "expert", [(m, m ^ 1) for m in range(members)])
+
+    def plane(x, k):
+        return lax.ppermute(x, "expert", [(m, m ^ (2 * k)) for m in range(members)])
+
+    info = jnp.concatenate([expert_ids.astype(F32).T, gate_weights.T], axis=0)
+    away = across(lax.dynamic_slice(tokens, (0, (1 - side) * half), (tok, half)))
+    info_y = across(info)
+    mine = lax.dynamic_slice(tokens, (0, side * half), (tok, half))
+    block0 = jnp.stack([mine, away])
+    info0 = jnp.stack([info, info_y])
+    wg_oth, wu_oth, wd_oth = cores(w_gate), cores(w_up), cores(w_down)
+    info_a = [info0] + [plane(info0, k) for k in range(1, planes)]
+    tok_a = [block0] + [plane(block0, k) for k in range(1, planes)]
+    info_flip = flip(jnp.stack(info_a))
+
+    kept = None
+    returned = []
+    for k in range(planes):
+        tok_b = flip(tok_a[k])
+        info_b = info_flip[k]
+        send, keep = call(
+            functools.partial(rows_kernel, cap, top),
+            "gate_up",
+            experts,
+            place,
+            [info_a[k], info_b, tok_a[k], tok_b],
+            [w_gate, wg_oth, w_up, wu_oth],
+            [],
+            [
+                jax.ShapeDtypeStruct((experts, both, 2 * hidden_width), BF16),
+                jax.ShapeDtypeStruct((experts, both, 2 * hidden_width), F32),
+            ],
+            [pltpu.VMEM((experts, 2 * both, half), BF16)],
+            4 * experts * 2 * both * half * hidden_width,
+        )
+        sums = keep + across(send).astype(F32)
+        gate_sum, up_sum = sums[..., :hidden_width], sums[..., hidden_width:]
+        hidden = (jax.nn.silu(gate_sum) * up_sum).astype(BF16)
+        hidden_par = across(hidden)
+        back, stay = call(
+            functools.partial(down_kernel, cap, top),
+            "down",
+            experts,
+            place,
+            [info_a[k], info_b],
+            [hidden, hidden_par, w_down, wd_oth],
+            [
+                jax.ShapeDtypeStruct((2, tok, half), BF16),
+                jax.ShapeDtypeStruct((2, tok, half), F32),
+            ],
+            [],
+            [pltpu.VMEM((2, experts * both, half), BF16)],
+            2 * experts * 2 * both * half * hidden_width,
+        )
+        part = stay + flip(back).astype(F32)
+        if k == 0:
+            kept = part
+        else:
+            returned.append(plane(part.astype(BF16), k))
+    total = kept
+    for r in returned:
+        total = total + r.astype(F32)
+    total = total.astype(BF16)
+    far = across(total[1])
+    near = total[0]
+    first = jnp.where(side == 0, near, far)
+    second = jnp.where(side == 0, far, near)
+    return jnp.concatenate([first, second], axis=1)
+
+
 def solution(mesh):
     in_specs = (
         P(("dp", "expert"), None),
@@ -69,6 +303,12 @@
         P("expert", None, "dp"),
     )
     out_specs = P(("dp", "expert"), None)
+    planes = mesh.shape["expert"] // 2
+    paired = mesh.shape["dp"] == 4 and planes >= 1 and planes & (planes - 1) == 0
     return jax.shard_map(
-        on_device, mesh=mesh, in_specs=in_specs, out_specs=out_specs, check_vma=False
-    )
+        local_weights if paired else gathered_weights,
+        mesh=mesh,
+        in_specs=in_specs,
+        out_specs=out_specs,
+        check_vma=False,
+    )

time: 381 us -> 227 us (0.60)
  waiting for transfers between devices: 223 us -> 97.3 us
  blocking collectives: 77.7 us -> 0 us
  Pallas kernels: 0 us -> 65 us
  starting transfers between devices: 5.72 us -> 49.6 us
  matrix products: 26.3 us -> 0 us
  local copies, waits for them, and re-layouts: 24.5 us -> 3.49 us
  between operations: 13.2 us -> 0.25 us
    all_gather x3 -> x0, waiting for transfers between devices: 150 us -> none  [the longest x1 83.7 us: on_device(): down_full = lax.all_gather(w_down, 'dp', axis=2, tiled=True)]
    ppermute x0 -> x32, waiting for transfers between devices: none -> 97.3 us  [the longest x9 50.8 us: plane(): return lax.ppermute(x, 'expert', [(m, m ^ 2 * k) for m in range(members)])]
    all_to_all x1 -> x0, blocking collectives: 77.7 us -> none  [on_device(): lax.all_to_all(outgoing, 'expert', split_axis=1, concat_axis=1, tiled=True)]
    all_to_all x1 -> x0, waiting for transfers between devices: 71.1 us -> none  [on_device(): lax.all_to_all(results.reshape(local_experts, members, capacity, model_wi...]
    pallas_call x0 -> x8, Pallas kernels: none -> 65 us  [call(): pl.pallas_call(kernel, name=name, out_shape=out_shape, grid_spec=pltpu.Pr...]
    ppermute x0 -> x32, starting transfers between devices: none -> 49.6 us  [the longest x9 23.9 us: plane(): return lax.ppermute(x, 'expert', [(m, m ^ 2 * k) for m in range(members)])]
    dot_general x2 -> x0, matrix products: 26.3 us -> none  [the longest x1 15.8 us: expert_layer(): jnp.einsum('erf,efd->erd', hidden, down_full, preferred_element_type=jnp....]
    gather x2 -> x0, local copies, waits for them, and re-layouts: 7.59 us -> none  [the longest x1 4.26 us: on_device(): tokens[source_row]]
  transfers between devices with their start and end apart: 4 -> 32, of which waited for: 3 -> 13; matrix products, arithmetic and copies ran while one was open for 7% -> 5% of each run, Pallas kernels for 0% -> 29%
where the time goes in v1:
time: 227 us; the launch traced here: 226 us
  waiting for transfers between devices  97.3 us (43%)
  Pallas kernels  65 us (29%)
  starting transfers between devices  49.6 us (22%)
  other arithmetic  10.4 us (5%)
  local copies, waits for them, and re-layouts  3.49 us (2%)
    pallas_call x8, Pallas kernels, call(): pl.pallas_call(kernel, name=name, out_shape=out_shape, grid_spec=pltpu.Pr...  65 us
    ppermute x9, waiting for transfers between devices, plane(): return lax.ppermute(x, 'expert', [(m, m ^ 2 * k) for m in range(members)])  50.8 us
    ppermute x11, waiting for transfers between devices, across(): return lax.ppermute(x, 'dp', [(d, d ^ 2) for d in range(4)])  29.2 us
    ppermute x9, starting transfers between devices, plane(): return lax.ppermute(x, 'expert', [(m, m ^ 2 * k) for m in range(members)])  23.9 us
    ppermute x9, waiting for transfers between devices, flip(): return lax.ppermute(x, 'expert', [(m, m ^ 1) for m in range(members)])  17.3 us
    ppermute x11, starting transfers between devices, across(): return lax.ppermute(x, 'dp', [(d, d ^ 2) for d in range(4)])  15.5 us
    ppermute x9, starting transfers between devices, flip(): return lax.ppermute(x, 'expert', [(m, m ^ 1) for m in range(members)])  9.69 us
    add x4, other arithmetic, local_weights(): sums = keep + across(send).astype(F32)  5.09 us
  transfers between devices with their start and end apart: 32, of which 13 were waited for; matrix products, arithmetic and copies ran while one was open for 5% of the time, Pallas kernels for 29%

profile of v1, /device:TPU:0, one launch (start us, length us, event | category | flops | bytes accessed | tf_op | source)
XLA Modules:
  0.0 226.0 jit_solution(1833242532738876997)
XLA Ops:
  1.6 3.0 %collective-permute-start.5 = (bf16[128,1024]{1,0:T(8,128)(2,1)S(1)}, bf16[128,1024]{1,0:T(8,128)(2,1)S(1)}, u32[]{:S(2)}, u32[]{:S(2)}) collective-permute-start(bf16[128,1024]{1,0:T(8,128)(2,1)S(1)} %get-tuple-element.40), channel_id=1, source_target_pairs={{0,16},{8,24},{16,0},{24,8},{1,17},{9,25},{17,1},{25,9},{2,18},{10... | collective-permute-start | bytes 786440 | tf_op jit(solution)/shard_map/ppermute | solution.py:219
  5.3 5.8 %collective-permute-done.5 = bf16[128,1024]{1,0:T(8,128)(2,1)S(1)} collective-permute-done((bf16[128,1024]{1,0:T(8,128)(2,1)S(1)}, bf16[128,1024]{1,0:T(8,128)(2,1)S(1)}, u32[]{:S(2)}, u32[]{:S(2)}) %collective-permute-start.5) | collective-permute-done | bytes 262176 | tf_op jit(solution)/shard_map/ppermute | solution.py:219
  12.0 3.8 %collective-permute-start.25 = (bf16[2,128,1024]{2,1,0:T(8,128)(2,1)}, bf16[2,128,1024]{2,1,0:T(8,128)(2,1)}, u32[]{:S(2)}, u32[]{:S(2)}) collective-permute-start(bf16[2,128,1024]{2,1,0:T(8,128)(2,1)} %pad_maximum_fusion.tok_a), channel_id=1, source_target_pairs={{0,6},{1,7},{2,4},{3,5},{4,2},{5,3},{6,0},{7,1},{8,14},{9,15},{10,... | collective-permute-start | bytes 1572872 | tf_op jit(solution)/shard_map/ppermute | solution.py:228
  15.9 1.6 collective-permute-start
  17.4 2.1 collective-permute-done
  20.5 7.2 %collective-permute-done.3.info_a = f32[2,8,128]{2,1,0:T(8,128)S(1)} collective-permute-done((f32[2,8,128]{2,1,0:T(8,128)S(1)}, f32[2,8,128]{2,1,0:T(8,128)S(1)}, u32[]{:S(2)}, u32[]{:S(2)}) %collective-permute-start.3) | collective-permute-done | bytes 8224 | tf_op jit(solution)/shard_map/ppermute | solution.py:228
  27.7 11.2 %collective-permute-start.1 = (f32[2,8,128]{2,1,0:T(8,128)S(1)}, f32[2,8,128]{2,1,0:T(8,128)S(1)}, u32[]{:S(2)}, u32[]{:S(2)}) collective-permute-start(f32[2,8,128]{2,1,0:T(8,128)S(1)} %get-tuple-element.46.info_a), channel_id=1, source_target_pairs={{0,2},{1,3},{2,0},{3,1},{4,6},{5,7},{6,4},{7,5},{8,10},{9,11},{10,... | collective-permute-start | bytes 24584 | tf_op jit(solution)/shard_map/ppermute | solution.py:228
  38.9 1.6 collective-permute-done.1.info_a
  42.1 3.0 %collective-permute-start.19 = (bf16[2,128,1024]{2,1,0:T(8,128)(2,1)}, bf16[2,128,1024]{2,1,0:T(8,128)(2,1)}, u32[]{:S(2)}, u32[]{:S(2)}) collective-permute-start(bf16[2,128,1024]{2,1,0:T(8,128)(2,1)} %pad_maximum_fusion.tok_a), channel_id=1, source_target_pairs={{0,4},{1,5},{2,6},{3,7},{4,0},{5,1},{6,2},{7,3},{8,12},{9,13},{10,... | collective-permute-start | bytes 1572872 | tf_op jit(solution)/shard_map/ppermute | solution.py:228
  45.1 1.6 collective-permute-start.13
  46.7 1.6 collective-permute-start.26
  49.0 17.4 %collective-permute-done.19.tok_a = bf16[2,128,1024]{2,1,0:T(8,128)(2,1)} collective-permute-done((bf16[2,128,1024]{2,1,0:T(8,128)(2,1)}, bf16[2,128,1024]{2,1,0:T(8,128)(2,1)}, u32[]{:S(2)}, u32[]{:S(2)}) %collective-permute-start.19) | collective-permute-done | bytes 524320 | tf_op jit(solution)/shard_map/ppermute | solution.py:228
  69.7 1.7 copy-done.1
  71.4 9.3 %gate_up.7 = (bf16[4,48,1536]{2,1,0:T(8,128)(2,1)}, f32[4,48,1536]{2,1,0:T(8,128)}) custom-call(s32[2]{0:T(128)} %pad_add_fusion.place, f32[2,8,128]{2,1,0:T(8,128)} %copy-done.16, f32[2,8,128]{2,1,0:T(8,128)} %get-tuple-element.42.info_b, bf16[2,128,1024]{2,1,0:T(8,128)(2,1)} %collective-permute-done.25.tok_a, ...), custom_call_target="tpu_custom_call" | custom-call | flops 1207959552 | bytes 15417344 | tf_op jit(solution)/shard_map/gate_up/pallas_call | solution.py:188
  80.7 1.6 collective-permute-start.27
  82.3 9.1 %gate_up.6 = (bf16[4,48,1536]{2,1,0:T(8,128)(2,1)}, f32[4,48,1536]{2,1,0:T(8,128)}) custom-call(s32[2]{0:T(128)} %pad_add_fusion.place, f32[2,8,128]{2,1,0:T(8,128)} %copy-done.15, f32[2,8,128]{2,1,0:T(8,128)} %get-tuple-element.43.info_b, bf16[2,128,1024]{2,1,0:T(8,128)(2,1)} %collective-permute-done.19.tok_a, ...), custom_call_target="tpu_custom_call" | custom-call | flops 1207959552 | bytes 15417344 | tf_op jit(solution)/shard_map/gate_up/pallas_call | solution.py:188
  92.7 9.1 %gate_up.5 = (bf16[4,48,1536]{2,1,0:T(8,128)(2,1)}, f32[4,48,1536]{2,1,0:T(8,128)}) custom-call(s32[2]{0:T(128)} %pad_add_fusion.place, f32[2,8,128]{2,1,0:T(8,128)} %copy-done.14, f32[2,8,128]{2,1,0:T(8,128)} %get-tuple-element.44.info_b, bf16[2,128,1024]{2,1,0:T(8,128)(2,1)} %collective-permute-done.13.tok_a, ...), custom_call_target="tpu_custom_call" | custom-call | flops 1207959552 | bytes 15417344 | tf_op jit(solution)/shard_map/gate_up/pallas_call | solution.py:188
  103.3 9.1 %gate_up.4 = (bf16[4,48,1536]{2,1,0:T(8,128)(2,1)}, f32[4,48,1536]{2,1,0:T(8,128)}) custom-call(s32[2]{0:T(128)} %pad_add_fusion.place, f32[2,8,128]{2,1,0:T(8,128)} %copy-done.13, f32[2,8,128]{2,1,0:T(8,128)} %get-tuple-element.41.info_b, bf16[2,128,1024]{2,1,0:T(8,128)(2,1)} %pad_maximum_fusion.tok_a, bf16[2,128,1024]{2,1,0:T(8,128)(2,1)} %collective-permute-done.6.tok_b, ...), custom_call_target="tpu_custom_call" | custom-call | flops 1207959552 | bytes 15417344 | tf_op jit(solution)/shard_map/gate_up/pallas_call | solution.py:188
  114.6 1.6 collective-permute-start.28
  118.8 1.7 collective-permute-done.15
  123.7 9.4 %collective-permute-done.9 = bf16[4,48,1536]{2,1,0:T(8,128)(2,1)S(1)} collective-permute-done((bf16[4,48,1536]{2,1,0:T(8,128)(2,1)}, bf16[4,48,1536]{2,1,0:T(8,128)(2,1)S(1)}, u32[]{:S(2)}, u32[]{:S(2)}) %collective-permute-start.9) | collective-permute-done | bytes 589856 | tf_op jit(solution)/shard_map/ppermute | solution.py:219
  134.2 5.3 %collective-permute-done.28.hid_par = bf16[4,48,768]{2,1,0:T(8,128)(2,1)} collective-permute-done((bf16[4,48,768]{2,1,0:T(8,128)(2,1)S(1)}, bf16[4,48,768]{2,1,0:T(8,128)(2,1)}, u32[]{:S(2)}, u32[]{:S(2)}) %collective-permute-start.28) | collective-permute-done | bytes 294944 | tf_op jit(solution)/shard_map/ppermute | solution.py:219
  139.5 7.1 %down.7 = (bf16[2,128,1024]{2,1,0:T(8,128)(2,1)}, f32[2,128,1024]{2,1,0:T(8,128)}) custom-call(s32[2]{0:T(128)} %pad_add_fusion.place, f32[2,8,128]{2,1,0:T(8,128)} %copy-done.16, f32[2,8,128]{2,1,0:T(8,128)} %get-tuple-element.42.info_b, bf16[4,48,768]{2,1,0:T(8,128)(2,1)} %copy-done.4, bf16[4,48,768]{2,1,0:T(8,128)(2,1)} %collective-permute-done.28.hid_par, ...), custom_call_target="tpu_custom_call" | custom-call | flops 603979776 | bytes 8470528 | tf_op jit(solution)/shard_map/down/pallas_call | solution.py:188
  149.4 7.1 %down.6 = (bf16[2,128,1024]{2,1,0:T(8,128)(2,1)}, f32[2,128,1024]{2,1,0:T(8,128)}) custom-call(s32[2]{0:T(128)} %pad_add_fusion.place, f32[2,8,128]{2,1,0:T(8,128)} %copy-done.15, f32[2,8,128]{2,1,0:T(8,128)} %get-tuple-element.43.info_b, bf16[4,48,768]{2,1,0:T(8,128)(2,1)} %copy-done.3, bf16[4,48,768]{2,1,0:T(8,128)(2,1)} %collective-permute-done.22.hid_par, ...), custom_call_target="tpu_custom_call" | custom-call | flops 603979776 | bytes 8470528 | tf_op jit(solution)/shard_map/down/pallas_call | solution.py:188
  157.0 7.1 %down.5 = (bf16[2,128,1024]{2,1,0:T(8,128)(2,1)}, f32[2,128,1024]{2,1,0:T(8,128)}) custom-call(s32[2]{0:T(128)} %pad_add_fusion.place, f32[2,8,128]{2,1,0:T(8,128)} %copy-done.14, f32[2,8,128]{2,1,0:T(8,128)} %get-tuple-element.44.info_b, bf16[4,48,768]{2,1,0:T(8,128)(2,1)} %fusion.2.hid_own, bf16[4,48,768]{2,1,0:T(8,128)(2,1)} %collective-permute-done.16.hid_par, ...), custom_call_target="tpu_custom_call" | custom-call | flops 603979776 | bytes 8470528 | tf_op jit(solution)/shard_map/down/pallas_call | solution.py:188
  165.6 7.1 %down.4 = (bf16[2,128,1024]{2,1,0:T(8,128)(2,1)}, f32[2,128,1024]{2,1,0:T(8,128)}) custom-call(s32[2]{0:T(128)} %pad_add_fusion.place, f32[2,8,128]{2,1,0:T(8,128)} %copy-done.13, f32[2,8,128]{2,1,0:T(8,128)} %get-tuple-element.41.info_b, bf16[4,48,768]{2,1,0:T(8,128)(2,1)} %copy-done.5, bf16[4,48,768]{2,1,0:T(8,128)(2,1)} %collective-permute-done.10.hid_par, ...), custom_call_target="tpu_custom_call" | custom-call | flops 603979776 | bytes 8470528 | tf_op jit(solution)/shard_map/down/pallas_call | solution.py:188
  173.4 2.6 %collective-permute-start.30 = (bf16[2,128,1024]{2,1,0:T(8,128)(2,1)S(1)}, bf16[2,128,1024]{2,1,0:T(8,128)(2,1)S(1)}, u32[]{:S(2)}, u32[]{:S(2)}) collective-permute-start(bf16[2,128,1024]{2,1,0:T(8,128)(2,1)S(1)} %add_convert_fusion.1), channel_id=1, source_target_pairs={{0,6},{1,7},{2,4},{3,5},{4,2},{5,3},{6,0},{7,1},{8,14},{9,15},{10,... | collective-permute-start | bytes 1572872 | tf_op jit(solution)/shard_map/ppermute | solution.py:228
  176.3 7.8 %collective-permute-done.17 = bf16[2,128,1024]{2,1,0:T(8,128)(2,1)S(1)} collective-permute-done((bf16[2,128,1024]{2,1,0:T(8,128)(2,1)}, bf16[2,128,1024]{2,1,0:T(8,128)(2,1)S(1)}, u32[]{:S(2)}, u32[]{:S(2)}) %collective-permute-start.17) | collective-permute-done | bytes 524320 | tf_op jit(solution)/shard_map/ppermute | solution.py:225
  184.8 8.8 %collective-permute-done.12 = bf16[2,128,1024]{2,1,0:T(8,128)(2,1)S(1)} collective-permute-done((bf16[2,128,1024]{2,1,0:T(8,128)(2,1)}, bf16[2,128,1024]{2,1,0:T(8,128)(2,1)S(1)}, u32[]{:S(2)}, u32[]{:S(2)}) %collective-permute-start.12) | collective-permute-done | bytes 524320 | tf_op jit(solution)/shard_map/ppermute | solution.py:225
  193.5 24.7 %collective-permute-done.24 = bf16[2,128,1024]{2,1,0:T(8,128)(2,1)S(1)} collective-permute-done((bf16[2,128,1024]{2,1,0:T(8,128)(2,1)S(1)}, bf16[2,128,1024]{2,1,0:T(8,128)(2,1)S(1)}, u32[]{:S(2)}, u32[]{:S(2)}) %collective-permute-start.24) | collective-permute-done | bytes 524320 | tf_op jit(solution)/shard_map/ppermute | solution.py:228
  218.7 1.6 collective-permute-start.31
  220.3 4.8 %collective-permute-done.31 = bf16[128,1024]{1,0:T(8,128)(2,1)S(1)} collective-permute-done((bf16[128,1024]{1,0:T(8,128)(2,1)S(1)}, bf16[128,1024]{1,0:T(8,128)(2,1)S(1)}, u32[]{:S(2)}, u32[]{:S(2)}) %collective-permute-start.31) | collective-permute-done | bytes 262176 | tf_op jit(solution)/shard_map/ppermute | solution.py:219
  (99 shorter events, 29.2 us)
Async XLA Ops:
  0.0 69.6 %collective-permute-start.7 = (bf16[4,512,768]{2,1,0:T(8,128)(2,1)}, bf16[4,512,768]{2,1,0:T(8,128)(2,1)S(1)}, u32[]{:S(2)}, u32[]{:S(2)}) collective-permute-start(bf16[4,512,768]{2,1,0:T(8,128)(2,1)} %wg_own.7), channel_id=1, source_target_pairs={{0,8},{8,0},{16,24},{24,16},{1,9},{9,1},{17,25},{25,17},{2,10},{10... | collective-permute-start | bytes 9437192 | tf_op jit(solution)/shard_map/ppermute | solution.py:222
  0.5 69.2 %collective-permute-start.8 = (bf16[4,512,768]{2,1,0:T(8,128)(2,1)}, bf16[4,512,768]{2,1,0:T(8,128)(2,1)}, u32[]{:S(2)}, u32[]{:S(2)}) collective-permute-start(bf16[4,512,768]{2,1,0:T(8,128)(2,1)} %wu_own.7), channel_id=1, source_target_pairs={{0,8},{8,0},{16,24},{24,16},{1,9},{9,1},{17,25},{25,17},{2,10},{10... | collective-permute-start | bytes 9437192 | tf_op jit(solution)/shard_map/ppermute | solution.py:222
  1.6 9.5 %collective-permute-start.5 = (bf16[128,1024]{1,0:T(8,128)(2,1)S(1)}, bf16[128,1024]{1,0:T(8,128)(2,1)S(1)}, u32[]{:S(2)}, u32[]{:S(2)}) collective-permute-start(bf16[128,1024]{1,0:T(8,128)(2,1)S(1)} %get-tuple-element.40), channel_id=1, source_target_pairs={{0,16},{8,24},{16,0},{24,8},{1,17},{9,25},{17,1},{25,9},{2,18},{10... | collective-permute-start | bytes 786440 | tf_op jit(solution)/shard_map/ppermute | solution.py:219
  12.0 34.7 %collective-permute-start.25 = (bf16[2,128,1024]{2,1,0:T(8,128)(2,1)}, bf16[2,128,1024]{2,1,0:T(8,128)(2,1)}, u32[]{:S(2)}, u32[]{:S(2)}) collective-permute-start(bf16[2,128,1024]{2,1,0:T(8,128)(2,1)} %pad_maximum_fusion.tok_a), channel_id=1, source_target_pairs={{0,6},{1,7},{2,4},{3,5},{4,2},{5,3},{6,0},{7,1},{8,14},{9,15},{10,... | collective-permute-start | bytes 1572872 | tf_op jit(solution)/shard_map/ppermute | solution.py:228
  15.9 3.7 %collective-permute-start = (f32[8,128]{1,0:T(8,128)S(1)}, f32[8,128]{1,0:T(8,128)S(1)}, u32[]{:S(2)}, u32[]{:S(2)}) collective-permute-start(f32[8,128]{1,0:T(8,128)S(1)} %get-tuple-element.48), channel_id=1, source_target_pairs={{0,16},{8,24},{16,0},{24,8},{1,17},{9,25},{17,1},{25,9},{2,18},{10... | collective-permute-start | bytes 12296 | tf_op jit(solution)/shard_map/ppermute | solution.py:219
  19.5 8.2 %collective-permute-start.3 = (f32[2,8,128]{2,1,0:T(8,128)S(1)}, f32[2,8,128]{2,1,0:T(8,128)S(1)}, u32[]{:S(2)}, u32[]{:S(2)}) collective-permute-start(f32[2,8,128]{2,1,0:T(8,128)S(1)} %get-tuple-element.46.info_a), channel_id=1, source_target_pairs={{0,6},{1,7},{2,4},{3,5},{4,2},{5,3},{6,0},{7,1},{8,14},{9,15},{10,... | collective-permute-start | bytes 24584 | tf_op jit(solution)/shard_map/ppermute | solution.py:228
  19.5 19.4 %collective-permute-start.2 = (f32[2,8,128]{2,1,0:T(8,128)S(1)}, f32[2,8,128]{2,1,0:T(8,128)S(1)}, u32[]{:S(2)}, u32[]{:S(2)}) collective-permute-start(f32[2,8,128]{2,1,0:T(8,128)S(1)} %get-tuple-element.46.info_a), channel_id=1, source_target_pairs={{0,4},{1,5},{2,6},{3,7},{4,0},{5,1},{6,2},{7,3},{8,12},{9,13},{10,... | collective-permute-start | bytes 24584 | tf_op jit(solution)/shard_map/ppermute | solution.py:228
  27.7 12.8 %collective-permute-start.1 = (f32[2,8,128]{2,1,0:T(8,128)S(1)}, f32[2,8,128]{2,1,0:T(8,128)S(1)}, u32[]{:S(2)}, u32[]{:S(2)}) collective-permute-start(f32[2,8,128]{2,1,0:T(8,128)S(1)} %get-tuple-element.46.info_a), channel_id=1, source_target_pairs={{0,2},{1,3},{2,0},{3,1},{4,6},{5,7},{6,4},{7,5},{8,10},{9,11},{10,... | collective-permute-start | bytes 24584 | tf_op jit(solution)/shard_map/ppermute | solution.py:228
  40.6 4.5 %collective-permute-start.4 = (f32[4,2,8,128]{3,2,1,0:T(8,128)S(1)}, f32[4,2,8,128]{3,2,1,0:T(8,128)S(1)}, u32[]{:S(2)}, u32[]{:S(2)}) collective-permute-start(f32[4,2,8,128]{3,2,1,0:T(8,128)S(1)} %pad_maximum_fusion.2), channel_id=1, source_target_pairs={{0,1},{1,0},{2,3},{3,2},{4,5},{5,4},{6,7},{7,6},{8,9},{9,8},{10,11... | collective-permute-start | bytes 98312 | tf_op jit(solution)/shard_map/ppermute | solution.py:225
  42.1 24.3 %collective-permute-start.19 = (bf16[2,128,1024]{2,1,0:T(8,128)(2,1)}, bf16[2,128,1024]{2,1,0:T(8,128)(2,1)}, u32[]{:S(2)}, u32[]{:S(2)}) collective-permute-start(bf16[2,128,1024]{2,1,0:T(8,128)(2,1)} %pad_maximum_fusion.tok_a), channel_id=1, source_target_pairs={{0,4},{1,5},{2,6},{3,7},{4,0},{5,1},{6,2},{7,3},{8,12},{9,13},{10,... | collective-permute-start | bytes 1572872 | tf_op jit(solution)/shard_map/ppermute | solution.py:228
  45.1 21.9 %collective-permute-start.13 = (bf16[2,128,1024]{2,1,0:T(8,128)(2,1)}, bf16[2,128,1024]{2,1,0:T(8,128)(2,1)}, u32[]{:S(2)}, u32[]{:S(2)}) collective-permute-start(bf16[2,128,1024]{2,1,0:T(8,128)(2,1)} %pad_maximum_fusion.tok_a), channel_id=1, source_target_pairs={{0,2},{1,3},{2,0},{3,1},{4,6},{5,7},{6,4},{7,5},{8,10},{9,11},{10,... | collective-permute-start | bytes 1572872 | tf_op jit(solution)/shard_map/ppermute | solution.py:228
  46.7 22.3 %collective-permute-start.26 = (bf16[2,128,1024]{2,1,0:T(8,128)(2,1)}, bf16[2,128,1024]{2,1,0:T(8,128)(2,1)}, u32[]{:S(2)}, u32[]{:S(2)}) collective-permute-start(bf16[2,128,1024]{2,1,0:T(8,128)(2,1)} %collective-permute-done.25.tok_a), channel_id=1, source_target_pairs={{0,1},{1,0},{2,3},{3,2},{4,5},{5,4},{6,7},{7,6},{8,9},{9,8},{10,11... | collective-permute-start | bytes 1572872 | tf_op jit(solution)/shard_map/ppermute | solution.py:225
  66.3 16.0 %collective-permute-start.20 = (bf16[2,128,1024]{2,1,0:T(8,128)(2,1)}, bf16[2,128,1024]{2,1,0:T(8,128)(2,1)}, u32[]{:S(2)}, u32[]{:S(2)}) collective-permute-start(bf16[2,128,1024]{2,1,0:T(8,128)(2,1)} %collective-permute-done.19.tok_a), channel_id=1, source_target_pairs={{0,1},{1,0},{2,3},{3,2},{4,5},{5,4},{6,7},{7,6},{8,9},{9,8},{10,11... | collective-permute-start | bytes 1572872 | tf_op jit(solution)/shard_map/ppermute | solution.py:225
  67.0 25.7 %collective-permute-start.14 = (bf16[2,128,1024]{2,1,0:T(8,128)(2,1)}, bf16[2,128,1024]{2,1,0:T(8,128)(2,1)}, u32[]{:S(2)}, u32[]{:S(2)}) collective-permute-start(bf16[2,128,1024]{2,1,0:T(8,128)(2,1)} %collective-permute-done.13.tok_a), channel_id=1, source_target_pairs={{0,1},{1,0},{2,3},{3,2},{4,5},{5,4},{6,7},{7,6},{8,9},{9,8},{10,11... | collective-permute-start | bytes 1572872 | tf_op jit(solution)/shard_map/ppermute | solution.py:225
  69.0 34.3 %collective-permute-start.6 = (bf16[2,128,1024]{2,1,0:T(8,128)(2,1)}, bf16[2,128,1024]{2,1,0:T(8,128)(2,1)}, u32[]{:S(2)}, u32[]{:S(2)}) collective-permute-start(bf16[2,128,1024]{2,1,0:T(8,128)(2,1)} %pad_maximum_fusion.tok_a), channel_id=1, source_target_pairs={{0,1},{1,0},{2,3},{3,2},{4,5},{5,4},{6,7},{7,6},{8,9},{9,8},{10,11... | collective-permute-start | bytes 1572872 | tf_op jit(solution)/shard_map/ppermute | solution.py:225
  80.7 32.1 %collective-permute-start.27 = (bf16[4,48,1536]{2,1,0:T(8,128)(2,1)}, bf16[4,48,1536]{2,1,0:T(8,128)(2,1)}, u32[]{:S(2)}, u32[]{:S(2)}) collective-permute-start(bf16[4,48,1536]{2,1,0:T(8,128)(2,1)} %get-tuple-element.34), channel_id=1, source_target_pairs={{0,16},{8,24},{16,0},{24,8},{1,17},{9,25},{17,1},{25,9},{2,18},{10... | collective-permute-start | bytes 1769480 | tf_op jit(solution)/shard_map/ppermute | solution.py:219
  82.3 51.9 %collective-permute-start.11 = (bf16[4,768,512]{2,1,0:T(8,128)(2,1)S(1)}, bf16[4,768,512]{2,1,0:T(8,128)(2,1)}, u32[]{:S(2)}, u32[]{:S(2)}) collective-permute-start(bf16[4,768,512]{2,1,0:T(8,128)(2,1)S(1)} %copy-done), channel_id=1, source_target_pairs={{0,8},{8,0},{16,24},{24,16},{1,9},{9,1},{17,25},{25,17},{2,10},{10... | collective-permute-start | bytes 9437192 | tf_op jit(solution)/shard_map/ppermute | solution.py:222
  91.4 24.8 %collective-permute-start.21 = (bf16[4,48,1536]{2,1,0:T(8,128)(2,1)}, bf16[4,48,1536]{2,1,0:T(8,128)(2,1)}, u32[]{:S(2)}, u32[]{:S(2)}) collective-permute-start(bf16[4,48,1536]{2,1,0:T(8,128)(2,1)} %get-tuple-element.30), channel_id=1, source_target_pairs={{0,16},{8,24},{16,0},{24,8},{1,17},{9,25},{17,1},{25,9},{2,18},{10... | collective-permute-start | bytes 1769480 | tf_op jit(solution)/shard_map/ppermute | solution.py:219
  101.8 18.8 %collective-permute-start.15 = (bf16[4,48,1536]{2,1,0:T(8,128)(2,1)}, bf16[4,48,1536]{2,1,0:T(8,128)(2,1)}, u32[]{:S(2)}, u32[]{:S(2)}) collective-permute-start(bf16[4,48,1536]{2,1,0:T(8,128)(2,1)} %get-tuple-element.26), channel_id=1, source_target_pairs={{0,16},{8,24},{16,0},{24,8},{1,17},{9,25},{17,1},{25,9},{2,18},{10... | collective-permute-start | bytes 1769480 | tf_op jit(solution)/shard_map/ppermute | solution.py:219
  112.4 20.7 %collective-permute-start.9 = (bf16[4,48,1536]{2,1,0:T(8,128)(2,1)}, bf16[4,48,1536]{2,1,0:T(8,128)(2,1)S(1)}, u32[]{:S(2)}, u32[]{:S(2)}) collective-permute-start(bf16[4,48,1536]{2,1,0:T(8,128)(2,1)} %get-tuple-element.22), channel_id=1, source_target_pairs={{0,16},{8,24},{16,0},{24,8},{1,17},{9,25},{17,1},{25,9},{2,18},{10... | collective-permute-start | bytes 1769480 | tf_op jit(solution)/shard_map/ppermute | solution.py:219
  114.6 24.9 %collective-permute-start.28 = (bf16[4,48,768]{2,1,0:T(8,128)(2,1)S(1)}, bf16[4,48,768]{2,1,0:T(8,128)(2,1)}, u32[]{:S(2)}, u32[]{:S(2)}) collective-permute-start(bf16[4,48,768]{2,1,0:T(8,128)(2,1)S(1)} %fusion.hid_own), channel_id=1, source_target_pairs={{0,16},{8,24},{16,0},{24,8},{1,17},{9,25},{17,1},{25,9},{2,18},{10... | collective-permute-start | bytes 884744 | tf_op jit(solution)/shard_map/ppermute | solution.py:219
  117.6 31.7 %collective-permute-start.22 = (bf16[4,48,768]{2,1,0:T(8,128)(2,1)S(1)}, bf16[4,48,768]{2,1,0:T(8,128)(2,1)}, u32[]{:S(2)}, u32[]{:S(2)}) collective-permute-start(bf16[4,48,768]{2,1,0:T(8,128)(2,1)S(1)} %fusion.1.hid_own), channel_id=1, source_target_pairs={{0,16},{8,24},{16,0},{24,8},{1,17},{9,25},{17,1},{25,9},{2,18},{10... | collective-permute-start | bytes 884744 | tf_op jit(solution)/shard_map/ppermute | solution.py:219
  122.6 34.4 %collective-permute-start.16 = (bf16[4,48,768]{2,1,0:T(8,128)(2,1)}, bf16[4,48,768]{2,1,0:T(8,128)(2,1)}, u32[]{:S(2)}, u32[]{:S(2)}) collective-permute-start(bf16[4,48,768]{2,1,0:T(8,128)(2,1)} %fusion.2.hid_own), channel_id=1, source_target_pairs={{0,16},{8,24},{16,0},{24,8},{1,17},{9,25},{17,1},{25,9},{2,18},{10... | collective-permute-start | bytes 884744 | tf_op jit(solution)/shard_map/ppermute | solution.py:219
  146.6 26.7 %collective-permute-start.29 = (bf16[2,128,1024]{2,1,0:T(8,128)(2,1)}, bf16[2,128,1024]{2,1,0:T(8,128)(2,1)S(1)}, u32[]{:S(2)}, u32[]{:S(2)}) collective-permute-start(bf16[2,128,1024]{2,1,0:T(8,128)(2,1)} %get-tuple-element.36), channel_id=1, source_target_pairs={{0,1},{1,0},{2,3},{3,2},{4,5},{5,4},{6,7},{7,6},{8,9},{9,8},{10,11... | collective-permute-start | bytes 1572872 | tf_op jit(solution)/shard_map/ppermute | solution.py:225
  148.2 17.5 %collective-permute-start.10 = (bf16[4,48,768]{2,1,0:T(8,128)(2,1)S(1)}, bf16[4,48,768]{2,1,0:T(8,128)(2,1)}, u32[]{:S(2)}, u32[]{:S(2)}) collective-permute-start(bf16[4,48,768]{2,1,0:T(8,128)(2,1)S(1)} %fusion.3.hid_own), channel_id=1, source_target_pairs={{0,16},{8,24},{16,0},{24,8},{1,17},{9,25},{17,1},{25,9},{2,18},{10... | collective-permute-start | bytes 884744 | tf_op jit(solution)/shard_map/ppermute | solution.py:219
  156.5 19.5 %collective-permute-start.23 = (bf16[2,128,1024]{2,1,0:T(8,128)(2,1)}, bf16[2,128,1024]{2,1,0:T(8,128)(2,1)S(1)}, u32[]{:S(2)}, u32[]{:S(2)}) collective-permute-start(bf16[2,128,1024]{2,1,0:T(8,128)(2,1)} %get-tuple-element.32), channel_id=1, source_target_pairs={{0,1},{1,0},{2,3},{3,2},{4,5},{5,4},{6,7},{7,6},{8,9},{9,8},{10,11... | collective-permute-start | bytes 1572872 | tf_op jit(solution)/shard_map/ppermute | solution.py:225
  164.1 20.0 %collective-permute-start.17 = (bf16[2,128,1024]{2,1,0:T(8,128)(2,1)}, bf16[2,128,1024]{2,1,0:T(8,128)(2,1)S(1)}, u32[]{:S(2)}, u32[]{:S(2)}) collective-permute-start(bf16[2,128,1024]{2,1,0:T(8,128)(2,1)} %get-tuple-element.28), channel_id=1, source_target_pairs={{0,1},{1,0},{2,3},{3,2},{4,5},{5,4},{6,7},{7,6},{8,9},{9,8},{10,11... | collective-permute-start | bytes 1572872 | tf_op jit(solution)/shard_map/ppermute | solution.py:225
  172.8 20.8 %collective-permute-start.12 = (bf16[2,128,1024]{2,1,0:T(8,128)(2,1)}, bf16[2,128,1024]{2,1,0:T(8,128)(2,1)S(1)}, u32[]{:S(2)}, u32[]{:S(2)}) collective-permute-start(bf16[2,128,1024]{2,1,0:T(8,128)(2,1)} %get-tuple-element.24), channel_id=1, source_target_pairs={{0,1},{1,0},{2,3},{3,2},{4,5},{5,4},{6,7},{7,6},{8,9},{9,8},{10,11... | collective-permute-start | bytes 1572872 | tf_op jit(solution)/shard_map/ppermute | solution.py:225
  173.4 20.1 %collective-permute-start.30 = (bf16[2,128,1024]{2,1,0:T(8,128)(2,1)S(1)}, bf16[2,128,1024]{2,1,0:T(8,128)(2,1)S(1)}, u32[]{:S(2)}, u32[]{:S(2)}) collective-permute-start(bf16[2,128,1024]{2,1,0:T(8,128)(2,1)S(1)} %add_convert_fusion.1), channel_id=1, source_target_pairs={{0,6},{1,7},{2,4},{3,5},{4,2},{5,3},{6,0},{7,1},{8,14},{9,15},{10,... | collective-permute-start | bytes 1572872 | tf_op jit(solution)/shard_map/ppermute | solution.py:228
  176.2 42.0 %collective-permute-start.24 = (bf16[2,128,1024]{2,1,0:T(8,128)(2,1)S(1)}, bf16[2,128,1024]{2,1,0:T(8,128)(2,1)S(1)}, u32[]{:S(2)}, u32[]{:S(2)}) collective-permute-start(bf16[2,128,1024]{2,1,0:T(8,128)(2,1)S(1)} %add_convert_fusion.2), channel_id=1, source_target_pairs={{0,4},{1,5},{2,6},{3,7},{4,0},{5,1},{6,2},{7,3},{8,12},{9,13},{10,... | collective-permute-start | bytes 1572872 | tf_op jit(solution)/shard_map/ppermute | solution.py:228
  184.2 34.0 %collective-permute-start.18 = (bf16[2,128,1024]{2,1,0:T(8,128)(2,1)S(1)}, bf16[2,128,1024]{2,1,0:T(8,128)(2,1)S(1)}, u32[]{:S(2)}, u32[]{:S(2)}) collective-permute-start(bf16[2,128,1024]{2,1,0:T(8,128)(2,1)S(1)} %add_convert_fusion.3), channel_id=1, source_target_pairs={{0,2},{1,3},{2,0},{3,1},{4,6},{5,7},{6,4},{7,5},{8,10},{9,11},{10,... | collective-permute-start | bytes 1572872 | tf_op jit(solution)/shard_map/ppermute | solution.py:228
  218.7 6.4 %collective-permute-start.31 = (bf16[128,1024]{1,0:T(8,128)(2,1)S(1)}, bf16[128,1024]{1,0:T(8,128)(2,1)S(1)}, u32[]{:S(2)}, u32[]{:S(2)}) collective-permute-start(bf16[128,1024]{1,0:T(8,128)(2,1)S(1)} %slice_bitcast_fusion), channel_id=1, source_target_pairs={{0,16},{8,24},{16,0},{24,8},{1,17},{9,25},{17,1},{25,9},{2,18},{10... | collective-permute-start | bytes 786440 | tf_op jit(solution)/shard_map/ppermute | solution.py:219
  (18 other events, 325.6 us)
